TPU v7x, 32 devices: a whole 2x2x4 slice. The times are simulated.
32 devices in a mesh: depth: 8 (over y, x, core), area: 4 (over z).
Axes of the slice: x: 2, y: 2, z: 4, core: 2. Of those that a mesh axis runs over, the one named last changes fastest.
Arguments:
- rhs_field: float32 [16, 32, 2048], P('depth', None, 'area'), may hold values from -8 to 8
- start_field: float32 [16, 32, 2048], P('depth', None, 'area'), may hold values from -4 to 4
- inverses: float32 [16, 2048, 512], P('depth', 'area'), may hold values from -0.044194174 to 1
- facies: int32 [16, 2048], P('depth', 'area'), may hold values from 0 to 7
- neighbours: int32 [2048, 4], P('area'), may hold values from 0 to 639, as said below
- lateral_table: float32 [8, 4], replicated, may hold values from 0.05 to 0.3
- vertical_table: float32 [8], replicated, may hold values from 0.9 to 1
Outputs:
- updated: float32 [16, 32, 2048], P('depth', None, 'area')
Inputs may be any that keep to these rules, and one draw needn't show every extreme that they name: `neighbours`: index 64 + c is column c itself; entries 0 and 1 of column c are c - 1 and c + 1, the others lie within 64 columns of c and differ from it.
All inputs are finite; a program needn't handle non-finite values.
Results may differ from a plain program's by a relative error of at most 0.00016.
Values sent between devices are 32-bit elements; how exact they have to be, the bound alone decides.
No kernel may reach another device: no remote copies, remote signals or barrier semaphores. Data moves between devices by JAX's collectives and lax.ppermute only.
A program may use at most 128 MiB of HBM per device.

v0:
```python
import jax
import jax.numpy as jnp
from jax import lax
from jax.sharding import PartitionSpec as P

HW = 64


def with_halo(block, sides, width):
    for axis, dim in sides:
        count = lax.axis_size(axis)
        forward = [(i, i + 1) for i in range(count - 1)]
        backward = [(target, source) for source, target in forward]
        low = lax.ppermute(
            lax.slice_in_dim(block, block.shape[dim] - width, None, axis=dim), axis, forward
        )
        high = lax.ppermute(lax.slice_in_dim(block, 0, width, axis=dim), axis, backward)
        block = jnp.concatenate([low, block, high], axis=dim)
    return block


def passed_along(value, axis, steps):
    count = lax.axis_size(axis)
    leading, last = (max(0, -steps), min(count, count - steps))
    return lax.ppermute(value, axis, [(source, source + steps) for source in range(leading, last)])


def times_block(field, block):
    return jnp.dot(field, block, precision=lax.Precision.HIGHEST)


def times_block_t(field, block):
    return jnp.einsum("rd,cd->rc", field, block, precision=lax.Precision.HIGHEST)


def shards(rhs_field, start_field, inverses, facies, neighbours, lateral_table, vertical_table):
    layers = rhs_field.shape[0]
    width = rhs_field.shape[2]
    count = rhs_field.shape[1]
    onehot = (facies[:, :, None] == jnp.arange(lateral_table.shape[0], dtype=jnp.int32)).astype(
        jnp.float32
    )
    lat_weight = jnp.sum(onehot[:, :, :, None] * lateral_table[None, None], axis=2)
    vert = jnp.sum(onehot * vertical_table[None, None], axis=2)

    def lateral(field, extended):
        values = extended[:, :, neighbours]
        return jnp.sum(lat_weight[:, None] * (field[..., None] - values), axis=-1)

    extended_start = with_halo(start_field, (("area", 2),), HW)
    from_below = passed_along(vert[0][None] * start_field[0], "depth", -1)
    upper = jnp.concatenate([vert[1:, None, :] * start_field[1:], from_below[None]], axis=0)
    g = rhs_field - lateral(start_field, extended_start) + upper

    def run_down(incoming):
        previous = incoming
        outs = []
        for layer in range(layers):
            previous = times_block(g[layer] + vert[layer][None] * previous, inverses[layer])
            outs.append(previous)
        return jnp.stack(outs, axis=0)

    zeros = jnp.zeros((count, width), jnp.float32)

    def down_step(index, incoming):
        last = run_down(incoming)[-1]
        return passed_along(last, "depth", 1)

    entering = lax.fori_loop(0, lax.axis_size("depth") - 1, down_step, zeros)
    sweep = run_down(entering)
    extended_sweep = with_halo(sweep, (("area", 2),), HW)
    shifted = jnp.concatenate([entering[None], sweep[:-1]], axis=0)
    h = rhs_field - lateral(sweep, extended_sweep) + vert[:, None, :] * shifted

    def run_up(incoming):
        carried = incoming
        outs = [None] * layers
        for layer in range(layers - 1, -1, -1):
            result = times_block_t(h[layer] + carried, inverses[layer])
            outs[layer] = result
            carried = vert[layer][None] * result
        return (jnp.stack(outs, axis=0), carried)

    def up_step(index, incoming):
        _, leaving = run_up(incoming)
        return passed_along(leaving, "depth", -1)

    arriving = lax.fori_loop(0, lax.axis_size("depth") - 1, up_step, zeros)
    updated, _ = run_up(arriving)
    return updated


def solution(mesh):
    return jax.shard_map(
        shards,
        mesh=mesh,
        in_specs=(
            P("depth", None, "area"),
            P("depth", None, "area"),
            P("depth", "area", None),
            P("depth", "area"),
            P("area", None),
            P(),
            P(),
        ),
        out_specs=P("depth", None, "area"),
        check_vma=False,
    )
```

profile of v0, /device:TPU:19, one launch (start us, length us, event | category | flops | bytes accessed | tf_op | source)
XLA Modules:
  0.0 185.1 jit_solution(1357948747082044513)
XLA Ops:
  1.7 2.6 %collective-permute-start.4 = (f32[32,512]{1,0:T(8,128)S(1)}, f32[32,512]{1,0:T(8,128)}, u32[]{:S(2)}, u32[]{:S(2)}) collective-permute-start(f32[32,512]{1,0:T(8,128)S(1)} %bitcast_multiply_fusion), channel_id=1, source_target_pairs={{4,0},{8,4},{12,8},{16,12},{20,16},{24,20},{28,24},{5,1},{9,5},{13... | collective-permute-start | bytes 196616 | tf_op jit(solution)/shard_map/ppermute | solution.py:25
  7.2 3.2 %collective-permute-start.2 = (f32[2,32,64]{2,1,0:T(8,128)S(1)}, f32[2,32,64]{2,1,0:T(8,128)S(1)}, u32[]{:S(2)}, u32[]{:S(2)}) collective-permute-start(f32[2,32,64]{2,1,0:T(8,128)S(1)} %get-tuple-element.87), channel_id=1, source_target_pairs={{0,1},{1,2},{2,3},{4,5},{5,6},{6,7},{8,9},{9,10},{10,11},{12,13},{... | collective-permute-start | bytes 49160 | tf_op jit(solution)/shard_map/ppermute | solution.py:14
  16.4 6.8 %gather_fusion = f32[2048,2,32]{2,1,0:T(2,128)S(1)} fusion(f32[2,32,640]{1,0,2:T(2,128)S(1)} %copy.32, s32[2048]{0:T(1024)S(1)} %broadcast_clamp_fusion), kind=kCustom, calls=%fused_computation | custom fusion | bytes 1056768 | tf_op jit(solution)/shard_map/gather | solution.py:47
  24.3 6.6 %multiply_reduce_fusion.1 = f32[2,32,512]{1,2,0:T(8,128)S(1)} fusion(f32[2,32,512,4]{1,3,2,0:T(4,128)S(1)} %bitcast.105, f32[2,32,512]{1,2,0:T(8,128)S(1)} %copy-done.1, f32[2,512,4]{2,1,0:T(8,128)S(1)} %copy.29), kind=kLoop, calls=%fused_computation.23 | loop fusion | flops 360448 | bytes 802816 | tf_op jit(solution)/shard_map/reduce_sum | solution.py:48
  31.9 54.7 %while.20 = (s32[]{:T(128)}, f32[32,512]{1,0:T(8,128)S(1)}, f32[2,32,512]{2,1,0:T(8,128)S(1)}, f32[2,512]{1,0:T(2,128)S(1)}, f32[2,512,512]{2,1,0:T(8,128)S(1)}, /*index=5*/s32[]{:T(128)}) while((s32[]{:T(128)}, f32[32,512]{1,0:T(8,128)S(1)}, f32[2,32,512]{2,1,0:T(8,128)S(1)}, f32[2,512]{1,0:T(2,128)S(1)}, f32[2,512,512]{2,1,0:T(8,128)S(1)}, ...), condition=%wide.region_4.0_spmd, body=%wide.region_3.0_spmd.sunk | while | flops 201392128 | bytes 2764909 | solution.py:69
  33.4 4.4 %collective-permute-start = (f32[32,512]{1,0:T(8,128)S(1)}, f32[32,512]{1,0:T(8,128)S(1)}, u32[]{:S(2)}, u32[]{:S(2)}) collective-permute-start(f32[32,512]{1,0:T(8,128)S(1)} %fusion.65), channel_id=1, source_target_pairs={{0,4},{4,8},{8,12},{12,16},{16,20},{20,24},{24,28},{1,5},{5,9},{9,... | collective-permute-start | bytes 196616 | tf_op jit(solution)/shard_map/while/body/eval_jaxpr/ppermute | solution.py:25
  40.6 5.2 %collective-permute-start = (f32[32,512]{1,0:T(8,128)S(1)}, f32[32,512]{1,0:T(8,128)S(1)}, u32[]{:S(2)}, u32[]{:S(2)}) collective-permute-start(f32[32,512]{1,0:T(8,128)S(1)} %fusion.65), channel_id=1, source_target_pairs={{0,4},{4,8},{8,12},{12,16},{16,20},{20,24},{24,28},{1,5},{5,9},{9,... | collective-permute-start | bytes 196616 | tf_op jit(solution)/shard_map/while/body/eval_jaxpr/ppermute | solution.py:25
  48.5 5.2 %collective-permute-start = (f32[32,512]{1,0:T(8,128)S(1)}, f32[32,512]{1,0:T(8,128)S(1)}, u32[]{:S(2)}, u32[]{:S(2)}) collective-permute-start(f32[32,512]{1,0:T(8,128)S(1)} %fusion.65), channel_id=1, source_target_pairs={{0,4},{4,8},{8,12},{12,16},{16,20},{20,24},{24,28},{1,5},{5,9},{9,... | collective-permute-start | bytes 196616 | tf_op jit(solution)/shard_map/while/body/eval_jaxpr/ppermute | solution.py:25
  56.4 5.2 %collective-permute-start = (f32[32,512]{1,0:T(8,128)S(1)}, f32[32,512]{1,0:T(8,128)S(1)}, u32[]{:S(2)}, u32[]{:S(2)}) collective-permute-start(f32[32,512]{1,0:T(8,128)S(1)} %fusion.65), channel_id=1, source_target_pairs={{0,4},{4,8},{8,12},{12,16},{16,20},{20,24},{24,28},{1,5},{5,9},{9,... | collective-permute-start | bytes 196616 | tf_op jit(solution)/shard_map/while/body/eval_jaxpr/ppermute | solution.py:25
  64.3 5.2 %collective-permute-start = (f32[32,512]{1,0:T(8,128)S(1)}, f32[32,512]{1,0:T(8,128)S(1)}, u32[]{:S(2)}, u32[]{:S(2)}) collective-permute-start(f32[32,512]{1,0:T(8,128)S(1)} %fusion.65), channel_id=1, source_target_pairs={{0,4},{4,8},{8,12},{12,16},{16,20},{20,24},{24,28},{1,5},{5,9},{9,... | collective-permute-start | bytes 196616 | tf_op jit(solution)/shard_map/while/body/eval_jaxpr/ppermute | solution.py:25
  72.2 5.2 %collective-permute-start = (f32[32,512]{1,0:T(8,128)S(1)}, f32[32,512]{1,0:T(8,128)S(1)}, u32[]{:S(2)}, u32[]{:S(2)}) collective-permute-start(f32[32,512]{1,0:T(8,128)S(1)} %fusion.65), channel_id=1, source_target_pairs={{0,4},{4,8},{8,12},{12,16},{16,20},{20,24},{24,28},{1,5},{5,9},{9,... | collective-permute-start | bytes 196616 | tf_op jit(solution)/shard_map/while/body/eval_jaxpr/ppermute | solution.py:25
  80.2 5.2 %collective-permute-start = (f32[32,512]{1,0:T(8,128)S(1)}, f32[32,512]{1,0:T(8,128)S(1)}, u32[]{:S(2)}, u32[]{:S(2)}) collective-permute-start(f32[32,512]{1,0:T(8,128)S(1)} %fusion.65), channel_id=1, source_target_pairs={{0,4},{4,8},{8,12},{12,16},{16,20},{20,24},{24,28},{1,5},{5,9},{9,... | collective-permute-start | bytes 196616 | tf_op jit(solution)/shard_map/while/body/eval_jaxpr/ppermute | solution.py:25
  88.1 2.1 %collective-permute-start.6 = (f32[2,32,64]{2,1,0:T(8,128)S(1)}, f32[2,32,64]{2,1,0:T(8,128)S(1)}, u32[]{:S(2)}, u32[]{:S(2)}) collective-permute-start(f32[2,32,64]{2,1,0:T(8,128)S(1)} %get-tuple-element.86), channel_id=1, source_target_pairs={{1,0},{2,1},{3,2},{5,4},{6,5},{7,6},{9,8},{10,9},{11,10},{13,12},{... | collective-permute-start | bytes 49160 | tf_op jit(solution)/shard_map/ppermute | solution.py:17
  90.2 3.4 %collective-permute-start.5 = (f32[2,32,64]{2,1,0:T(8,128)S(1)}, f32[2,32,64]{2,1,0:T(8,128)S(1)}, u32[]{:S(2)}, u32[]{:S(2)}) collective-permute-start(f32[2,32,64]{2,1,0:T(8,128)S(1)} %get-tuple-element.85), channel_id=1, source_target_pairs={{0,1},{1,2},{2,3},{4,5},{5,6},{6,7},{8,9},{9,10},{10,11},{12,13},{... | collective-permute-start | bytes 49160 | tf_op jit(solution)/shard_map/ppermute | solution.py:14
  96.9 14.5 %gather_fusion.1 = f32[2048,2,32]{2,1,0:T(2,128)} fusion(f32[2,32,640]{1,0,2:T(2,128)S(1)} %copy.36, s32[2048]{0:T(1024)S(1)} %broadcast_clamp_fusion), kind=kCustom, calls=%fused_computation.1 | custom fusion | bytes 1056768 | tf_op jit(solution)/shard_map/gather | solution.py:47
  113.2 6.6 %multiply_reduce_fusion = f32[2,32,512]{1,2,0:T(8,128)S(1)} fusion(f32[2,32,512,4]{1,3,2,0:T(4,128)S(1)} %bitcast.104, f32[2,32,512]{1,2,0:T(8,128)S(1)} %copy-done.2, f32[2,512,4]{2,1,0:T(8,128)S(1)} %copy.29), kind=kLoop, calls=%fused_computation.22 | loop fusion | flops 360448 | bytes 802816 | tf_op jit(solution)/shard_map/reduce_sum | solution.py:48
  120.0 62.3 %while.21 = (s32[]{:T(128)}, f32[32,512]{1,0:T(8,128)S(1)}, f32[2,512]{1,0:T(2,128)S(1)}, f32[2,32,512]{2,1,0:T(8,128)S(1)}, f32[2,512,512]{2,1,0:T(8,128)S(1)}, /*index=5*/s32[]{:T(128)}) while((s32[]{:T(128)}, f32[32,512]{1,0:T(8,128)S(1)}, f32[2,512]{1,0:T(2,128)S(1)}, f32[2,32,512]{2,1,0:T(8,128)S(1)}, f32[2,512,512]{2,1,0:T(8,128)S(1)}, ...), condition=%wide.region_7.0_spmd, body=%wide.region_6.0_spmd.sunk | while | flops 201392128 | bytes 2764909 | solution.py:88
  124.1 6.6 %collective-permute-done.1 = f32[32,512]{1,0:T(8,128)S(1)} collective-permute-done((f32[32,512]{1,0:T(8,128)S(1)}, f32[32,512]{1,0:T(8,128)S(1)}, u32[]{:S(2)}, u32[]{:S(2)}) %collective-permute-start.1) | collective-permute-done | bytes 65568 | tf_op jit(solution)/shard_map/while/body/eval_jaxpr/ppermute | solution.py:25
  134.7 4.6 %collective-permute-done.1 = f32[32,512]{1,0:T(8,128)S(1)} collective-permute-done((f32[32,512]{1,0:T(8,128)S(1)}, f32[32,512]{1,0:T(8,128)S(1)}, u32[]{:S(2)}, u32[]{:S(2)}) %collective-permute-start.1) | collective-permute-done | bytes 65568 | tf_op jit(solution)/shard_map/while/body/eval_jaxpr/ppermute | solution.py:25
  143.3 4.6 %collective-permute-done.1 = f32[32,512]{1,0:T(8,128)S(1)} collective-permute-done((f32[32,512]{1,0:T(8,128)S(1)}, f32[32,512]{1,0:T(8,128)S(1)}, u32[]{:S(2)}, u32[]{:S(2)}) %collective-permute-start.1) | collective-permute-done | bytes 65568 | tf_op jit(solution)/shard_map/while/body/eval_jaxpr/ppermute | solution.py:25
  151.9 4.6 %collective-permute-done.1 = f32[32,512]{1,0:T(8,128)S(1)} collective-permute-done((f32[32,512]{1,0:T(8,128)S(1)}, f32[32,512]{1,0:T(8,128)S(1)}, u32[]{:S(2)}, u32[]{:S(2)}) %collective-permute-start.1) | collective-permute-done | bytes 65568 | tf_op jit(solution)/shard_map/while/body/eval_jaxpr/ppermute | solution.py:25
  160.5 4.6 %collective-permute-done.1 = f32[32,512]{1,0:T(8,128)S(1)} collective-permute-done((f32[32,512]{1,0:T(8,128)S(1)}, f32[32,512]{1,0:T(8,128)S(1)}, u32[]{:S(2)}, u32[]{:S(2)}) %collective-permute-start.1) | collective-permute-done | bytes 65568 | tf_op jit(solution)/shard_map/while/body/eval_jaxpr/ppermute | solution.py:25
  169.1 4.6 %collective-permute-done.1 = f32[32,512]{1,0:T(8,128)S(1)} collective-permute-done((f32[32,512]{1,0:T(8,128)S(1)}, f32[32,512]{1,0:T(8,128)S(1)}, u32[]{:S(2)}, u32[]{:S(2)}) %collective-permute-start.1) | collective-permute-done | bytes 65568 | tf_op jit(solution)/shard_map/while/body/eval_jaxpr/ppermute | solution.py:25
  177.8 4.6 %collective-permute-done.1 = f32[32,512]{1,0:T(8,128)S(1)} collective-permute-done((f32[32,512]{1,0:T(8,128)S(1)}, f32[32,512]{1,0:T(8,128)S(1)}, u32[]{:S(2)}, u32[]{:S(2)}) %collective-permute-start.1) | collective-permute-done | bytes 65568 | tf_op jit(solution)/shard_map/while/body/eval_jaxpr/ppermute | solution.py:25
  (111 shorter events, 69.3 us)
Async XLA Ops:
  0.0 16.0 %copy-start.3 = (f32[2,32,512]{2,1,0:T(8,128)S(1)}, f32[2,32,512]{2,1,0:T(8,128)}, u32[]{:S(2)}) copy-start(f32[2,32,512]{2,1,0:T(8,128)} %param.12) | copy-start | bytes 393220
  0.8 11.1 %copy-start.6 = (f32[1,512]{1,0:T(1,128)}, f32[1,512]{1,0:T(1,128)S(1)}, u32[]{:S(2)}) copy-start(f32[1,512]{1,0:T(1,128)S(1)} %get-tuple-element.90) | copy-start | bytes 6148
  1.7 29.3 %collective-permute-start.4 = (f32[32,512]{1,0:T(8,128)S(1)}, f32[32,512]{1,0:T(8,128)}, u32[]{:S(2)}, u32[]{:S(2)}) collective-permute-start(f32[32,512]{1,0:T(8,128)S(1)} %bitcast_multiply_fusion), channel_id=1, source_target_pairs={{4,0},{8,4},{12,8},{16,12},{20,16},{24,20},{28,24},{5,1},{9,5},{13... | collective-permute-start | bytes 196616 | tf_op jit(solution)/shard_map/ppermute | solution.py:25
  5.1 10.8 %collective-permute-start.3 = (f32[2,32,64]{2,1,0:T(8,128)S(1)}, f32[2,32,64]{2,1,0:T(8,128)S(1)}, u32[]{:S(2)}, u32[]{:S(2)}) collective-permute-start(f32[2,32,64]{2,1,0:T(8,128)S(1)} %get-tuple-element.88), channel_id=1, source_target_pairs={{1,0},{2,1},{3,2},{5,4},{6,5},{7,6},{9,8},{10,9},{11,10},{13,12},{... | collective-permute-start | bytes 49160 | tf_op jit(solution)/shard_map/ppermute | solution.py:17
  7.2 8.7 %collective-permute-start.2 = (f32[2,32,64]{2,1,0:T(8,128)S(1)}, f32[2,32,64]{2,1,0:T(8,128)S(1)}, u32[]{:S(2)}, u32[]{:S(2)}) collective-permute-start(f32[2,32,64]{2,1,0:T(8,128)S(1)} %get-tuple-element.87), channel_id=1, source_target_pairs={{0,1},{1,2},{2,3},{4,5},{5,6},{6,7},{8,9},{9,10},{10,11},{12,13},{... | collective-permute-start | bytes 49160 | tf_op jit(solution)/shard_map/ppermute | solution.py:14
  24.3 7.7 %copy-start = (f32[2,512,512]{2,1,0:T(8,128)S(1)}, f32[2,512,512]{2,1,0:T(8,128)}, u32[]{:S(2)}) copy-start(f32[2,512,512]{2,1,0:T(8,128)} %param.13) | copy-start | bytes 6291460
  31.9 54.7 %copy-start.7 = (f32[1,512]{1,0:T(1,128)S(1)}, f32[1,512]{1,0:T(1,128)}, u32[]{:S(2)}) copy-start(f32[1,512]{1,0:T(1,128)} %copy-done.6) | copy-start | bytes 6148
  33.4 5.8 %collective-permute-start = (f32[32,512]{1,0:T(8,128)S(1)}, f32[32,512]{1,0:T(8,128)S(1)}, u32[]{:S(2)}, u32[]{:S(2)}) collective-permute-start(f32[32,512]{1,0:T(8,128)S(1)} %fusion.65), channel_id=1, source_target_pairs={{0,4},{4,8},{8,12},{12,16},{16,20},{20,24},{24,28},{1,5},{5,9},{9,... | collective-permute-start | bytes 196616 | tf_op jit(solution)/shard_map/while/body/eval_jaxpr/ppermute | solution.py:25
  40.6 6.5 %collective-permute-start = (f32[32,512]{1,0:T(8,128)S(1)}, f32[32,512]{1,0:T(8,128)S(1)}, u32[]{:S(2)}, u32[]{:S(2)}) collective-permute-start(f32[32,512]{1,0:T(8,128)S(1)} %fusion.65), channel_id=1, source_target_pairs={{0,4},{4,8},{8,12},{12,16},{16,20},{20,24},{24,28},{1,5},{5,9},{9,... | collective-permute-start | bytes 196616 | tf_op jit(solution)/shard_map/while/body/eval_jaxpr/ppermute | solution.py:25
  48.5 6.5 %collective-permute-start = (f32[32,512]{1,0:T(8,128)S(1)}, f32[32,512]{1,0:T(8,128)S(1)}, u32[]{:S(2)}, u32[]{:S(2)}) collective-permute-start(f32[32,512]{1,0:T(8,128)S(1)} %fusion.65), channel_id=1, source_target_pairs={{0,4},{4,8},{8,12},{12,16},{16,20},{20,24},{24,28},{1,5},{5,9},{9,... | collective-permute-start | bytes 196616 | tf_op jit(solution)/shard_map/while/body/eval_jaxpr/ppermute | solution.py:25
  56.4 6.5 %collective-permute-start = (f32[32,512]{1,0:T(8,128)S(1)}, f32[32,512]{1,0:T(8,128)S(1)}, u32[]{:S(2)}, u32[]{:S(2)}) collective-permute-start(f32[32,512]{1,0:T(8,128)S(1)} %fusion.65), channel_id=1, source_target_pairs={{0,4},{4,8},{8,12},{12,16},{16,20},{20,24},{24,28},{1,5},{5,9},{9,... | collective-permute-start | bytes 196616 | tf_op jit(solution)/shard_map/while/body/eval_jaxpr/ppermute | solution.py:25
  64.3 6.5 %collective-permute-start = (f32[32,512]{1,0:T(8,128)S(1)}, f32[32,512]{1,0:T(8,128)S(1)}, u32[]{:S(2)}, u32[]{:S(2)}) collective-permute-start(f32[32,512]{1,0:T(8,128)S(1)} %fusion.65), channel_id=1, source_target_pairs={{0,4},{4,8},{8,12},{12,16},{16,20},{20,24},{24,28},{1,5},{5,9},{9,... | collective-permute-start | bytes 196616 | tf_op jit(solution)/shard_map/while/body/eval_jaxpr/ppermute | solution.py:25
  72.2 6.5 %collective-permute-start = (f32[32,512]{1,0:T(8,128)S(1)}, f32[32,512]{1,0:T(8,128)S(1)}, u32[]{:S(2)}, u32[]{:S(2)}) collective-permute-start(f32[32,512]{1,0:T(8,128)S(1)} %fusion.65), channel_id=1, source_target_pairs={{0,4},{4,8},{8,12},{12,16},{16,20},{20,24},{24,28},{1,5},{5,9},{9,... | collective-permute-start | bytes 196616 | tf_op jit(solution)/shard_map/while/body/eval_jaxpr/ppermute | solution.py:25
  80.2 6.5 %collective-permute-start = (f32[32,512]{1,0:T(8,128)S(1)}, f32[32,512]{1,0:T(8,128)S(1)}, u32[]{:S(2)}, u32[]{:S(2)}) collective-permute-start(f32[32,512]{1,0:T(8,128)S(1)} %fusion.65), channel_id=1, source_target_pairs={{0,4},{4,8},{8,12},{12,16},{16,20},{20,24},{24,28},{1,5},{5,9},{9,... | collective-permute-start | bytes 196616 | tf_op jit(solution)/shard_map/while/body/eval_jaxpr/ppermute | solution.py:25
  88.1 6.5 %collective-permute-start.6 = (f32[2,32,64]{2,1,0:T(8,128)S(1)}, f32[2,32,64]{2,1,0:T(8,128)S(1)}, u32[]{:S(2)}, u32[]{:S(2)}) collective-permute-start(f32[2,32,64]{2,1,0:T(8,128)S(1)} %get-tuple-element.86), channel_id=1, source_target_pairs={{1,0},{2,1},{3,2},{5,4},{6,5},{7,6},{9,8},{10,9},{11,10},{13,12},{... | collective-permute-start | bytes 49160 | tf_op jit(solution)/shard_map/ppermute | solution.py:17
  90.2 4.7 %collective-permute-start.5 = (f32[2,32,64]{2,1,0:T(8,128)S(1)}, f32[2,32,64]{2,1,0:T(8,128)S(1)}, u32[]{:S(2)}, u32[]{:S(2)}) collective-permute-start(f32[2,32,64]{2,1,0:T(8,128)S(1)} %get-tuple-element.85), channel_id=1, source_target_pairs={{0,1},{1,2},{2,3},{4,5},{5,6},{6,7},{8,9},{9,10},{10,11},{12,13},{... | collective-permute-start | bytes 49160 | tf_op jit(solution)/shard_map/ppermute | solution.py:14
  113.2 6.8 %copy-start.5 = (f32[2,32,512]{2,1,0:T(8,128)S(1)}, f32[2,32,512]{2,1,0:T(8,128)}, u32[]{:S(2)}) copy-start(f32[2,32,512]{2,1,0:T(8,128)} %param.11) | copy-start | bytes 393220
  122.1 8.5 %collective-permute-start.1 = (f32[32,512]{1,0:T(8,128)S(1)}, f32[32,512]{1,0:T(8,128)S(1)}, u32[]{:S(2)}, u32[]{:S(2)}) collective-permute-start(f32[32,512]{1,0:T(8,128)S(1)} %convolution_multiply_fusion.4), channel_id=1, source_target_pairs={{4,0},{8,4},{12,8},{16,12},{20,16},{24,20},{28,24},{5,1},{9,5},{13... | collective-permute-start | bytes 196616 | tf_op jit(solution)/shard_map/while/body/eval_jaxpr/ppermute | solution.py:25
  132.8 6.5 %collective-permute-start.1 = (f32[32,512]{1,0:T(8,128)S(1)}, f32[32,512]{1,0:T(8,128)S(1)}, u32[]{:S(2)}, u32[]{:S(2)}) collective-permute-start(f32[32,512]{1,0:T(8,128)S(1)} %convolution_multiply_fusion.4), channel_id=1, source_target_pairs={{4,0},{8,4},{12,8},{16,12},{20,16},{24,20},{28,24},{5,1},{9,5},{13... | collective-permute-start | bytes 196616 | tf_op jit(solution)/shard_map/while/body/eval_jaxpr/ppermute | solution.py:25
  141.4 6.5 %collective-permute-start.1 = (f32[32,512]{1,0:T(8,128)S(1)}, f32[32,512]{1,0:T(8,128)S(1)}, u32[]{:S(2)}, u32[]{:S(2)}) collective-permute-start(f32[32,512]{1,0:T(8,128)S(1)} %convolution_multiply_fusion.4), channel_id=1, source_target_pairs={{4,0},{8,4},{12,8},{16,12},{20,16},{24,20},{28,24},{5,1},{9,5},{13... | collective-permute-start | bytes 196616 | tf_op jit(solution)/shard_map/while/body/eval_jaxpr/ppermute | solution.py:25
  150.0 6.5 %collective-permute-start.1 = (f32[32,512]{1,0:T(8,128)S(1)}, f32[32,512]{1,0:T(8,128)S(1)}, u32[]{:S(2)}, u32[]{:S(2)}) collective-permute-start(f32[32,512]{1,0:T(8,128)S(1)} %convolution_multiply_fusion.4), channel_id=1, source_target_pairs={{4,0},{8,4},{12,8},{16,12},{20,16},{24,20},{28,24},{5,1},{9,5},{13... | collective-permute-start | bytes 196616 | tf_op jit(solution)/shard_map/while/body/eval_jaxpr/ppermute | solution.py:25
  158.6 6.5 %collective-permute-start.1 = (f32[32,512]{1,0:T(8,128)S(1)}, f32[32,512]{1,0:T(8,128)S(1)}, u32[]{:S(2)}, u32[]{:S(2)}) collective-permute-start(f32[32,512]{1,0:T(8,128)S(1)} %convolution_multiply_fusion.4), channel_id=1, source_target_pairs={{4,0},{8,4},{12,8},{16,12},{20,16},{24,20},{28,24},{5,1},{9,5},{13... | collective-permute-start | bytes 196616 | tf_op jit(solution)/shard_map/while/body/eval_jaxpr/ppermute | solution.py:25
  167.2 6.5 %collective-permute-start.1 = (f32[32,512]{1,0:T(8,128)S(1)}, f32[32,512]{1,0:T(8,128)S(1)}, u32[]{:S(2)}, u32[]{:S(2)}) collective-permute-start(f32[32,512]{1,0:T(8,128)S(1)} %convolution_multiply_fusion.4), channel_id=1, source_target_pairs={{4,0},{8,4},{12,8},{16,12},{20,16},{24,20},{28,24},{5,1},{9,5},{13... | collective-permute-start | bytes 196616 | tf_op jit(solution)/shard_map/while/body/eval_jaxpr/ppermute | solution.py:25
  175.8 6.5 %collective-permute-start.1 = (f32[32,512]{1,0:T(8,128)S(1)}, f32[32,512]{1,0:T(8,128)S(1)}, u32[]{:S(2)}, u32[]{:S(2)}) collective-permute-start(f32[32,512]{1,0:T(8,128)S(1)} %convolution_multiply_fusion.4), channel_id=1, source_target_pairs={{4,0},{8,4},{12,8},{16,12},{20,16},{24,20},{28,24},{5,1},{9,5},{13... | collective-permute-start | bytes 196616 | tf_op jit(solution)/shard_map/while/body/eval_jaxpr/ppermute | solution.py:25
  (3 other events, 9.6 us)
where the time goes:
time: 186 us; the launch traced here: 185 us
  starting transfers between devices  62.2 us (33%)
  waiting for transfers between devices  43.3 us (23%)
  local copies, waits for them, and re-layouts  30.4 us (16%)
  matrix products  28.1 us (15%)
  other arithmetic  20.4 us (11%)
    ppermute x15, starting transfers between devices, passed_along(): lax.ppermute(value, axis, [(source, source + steps) for source in range(l...  51.4 us
    ppermute x15, waiting for transfers between devices, passed_along(): lax.ppermute(value, axis, [(source, source + steps) for source in range(l...  43.1 us
    gather x4, local copies, waits for them, and re-layouts, lateral(): values = extended[:, :, neighbours]  23.3 us
    dot_general x16, matrix products, times_block_t(): jnp.einsum('rd,cd->rc', field, block, precision=lax.Precision.HIGHEST)  16.8 us
    reduce_sum x2, other arithmetic, lateral(): return jnp.sum(lat_weight[:, None] * (field[..., None] - values), axis=-1)  13.1 us
    dot_general x16, matrix products, times_block(): return jnp.dot(field, block, precision=lax.Precision.HIGHEST)  11.3 us
    ppermute x2, starting transfers between devices, with_halo(): lax.ppermute(lax.slice_in_dim(block, block.shape[dim] - width, None, axis...  6.58 us
    ppermute x2, starting transfers between devices, with_halo(): lax.ppermute(lax.slice_in_dim(block, 0, width, axis=dim), axis, backward)  4.15 us
  transfers between devices with their start and end apart: 19, of which 15 were waited for; matrix products, arithmetic and copies ran while one was open for 12% of the time, Pallas kernels for 0%

commit v1 on v0

v1 whole, which is shorter than its diff:
```python
import functools

import jax
import jax.numpy as jnp
from jax import lax
from jax.experimental import pallas as pl
from jax.experimental.pallas import tpu as pltpu
from jax.sharding import PartitionSpec as P

F32 = jnp.float32
BF16 = jnp.bfloat16
HW = 64
LANES = 128
NN = (((1,), (0,)), ((), ()))
NT = (((1,), (1,)), ((), ()))

VMEM = pl.BlockSpec(memory_space=pltpu.VMEM)
SMEM = pl.BlockSpec(memory_space=pltpu.SMEM)


def call(body, name, out_shape, in_specs, limit, flops, moved, scratch=()):
    return pl.pallas_call(
        body,
        name=name,
        out_shape=out_shape,
        in_specs=in_specs,
        out_specs=jax.tree.map(lambda _: VMEM, out_shape),
        scratch_shapes=list(scratch),
        compiler_params=pltpu.CompilerParams(vmem_limit_bytes=limit << 20),
        cost_estimate=pl.CostEstimate(flops=flops, bytes_accessed=moved, transcendentals=0),
    )


def sds(shape, dtype=F32):
    return jax.ShapeDtypeStruct(shape, dtype)


def split(value):
    high = value.astype(BF16)
    return high, (value - high.astype(F32)).astype(BF16)


def times(value, high, low, dims=NN):
    rows = value.shape[0]
    value_high, value_low = split(value)
    both = lax.dot_general(
        jnp.concatenate([value_high, value_low], axis=0), high, dims, preferred_element_type=F32
    )
    rest = lax.dot_general(value_high, low, dims, preferred_element_type=F32)
    return both[:rows] + (both[rows:] + rest)


def looked_up(kinds, entry, count):
    value = jnp.full(kinds.shape, entry(0), F32)
    for kind in range(1, count):
        value = jnp.where(kinds == kind, entry(kind), value)
    return value


def edges_kernel(start_ref, facies_ref, vertical_ref, left_ref, right_ref, top_ref):
    layers, _, width = start_ref.shape
    left_ref[...] = jnp.concatenate([start_ref[k, :, :HW] for k in range(layers)], axis=1)
    right_ref[...] = jnp.concatenate([start_ref[k, :, width - HW :] for k in range(layers)], axis=1)
    vert = looked_up(facies_ref[0:1, :], lambda kind: vertical_ref[kind], vertical_ref.shape[0])
    top_ref[...] = vert * start_ref[0]


def setup_kernel(inverses_ref, facies_ref, lateral_ref, vertical_ref,
                 high_ref, low_ref, product_ref, product_high_ref, product_low_ref,
                 weight_ref, vert_ref):
    layers, width, _ = inverses_ref.shape
    kinds = facies_ref[...]
    vert = looked_up(kinds, lambda kind: vertical_ref[kind], vertical_ref.shape[0])
    vert_ref[...] = vert
    for slot in range(lateral_ref.shape[1]):
        weight_ref[slot] = looked_up(kinds, lambda kind: lateral_ref[kind, slot], lateral_ref.shape[0])
    step = LANES
    for layer in range(layers):
        for row in range(0, width, step):
            rows = slice(row, row + step)
            high_ref[layer, rows, :], low_ref[layer, rows, :] = split(inverses_ref[layer, rows, :])
    for row in range(0, width, step):
        rows = slice(row, row + step)
        value = inverses_ref[0, rows, :]
        for layer in range(1, layers):
            value = times(value * vert[layer : layer + 1], high_ref[layer], low_ref[layer])
        scale = jnp.transpose(jnp.broadcast_to(vert[0:1, rows], (step, step)))
        value = value * jnp.concatenate([scale] * (width // step), axis=1)
        product_ref[rows, :] = value
        product_high_ref[rows, :], product_low_ref[rows, :] = split(value)


def pair_kernel(bit_of, own_ref, own_high_ref, own_low_ref, other_ref,
                other_high_ref, other_low_ref, product_ref, product_high_ref, product_low_ref):
    width = own_ref.shape[0]
    step = LANES
    for row in range(0, width, step):
        rows = slice(row, row + step)
        other_high_ref[rows, :], other_low_ref[rows, :] = split(other_ref[rows, :])
    upper = bit_of()

    def multiply(left_ref, right_high_ref, right_low_ref):
        for row in range(0, width, step):
            rows = slice(row, row + step)
            value = times(left_ref[rows, :], right_high_ref[...], right_low_ref[...])
            product_ref[rows, :] = value
            product_high_ref[rows, :], product_low_ref[rows, :] = split(value)

    @pl.when(upper == 1)
    def _():
        multiply(other_ref, own_high_ref, own_low_ref)

    @pl.when(upper == 0)
    def _():
        multiply(own_ref, other_high_ref, other_low_ref)


def split_kernel(value_ref, high_ref, low_ref):
    for row in range(0, value_ref.shape[0], LANES):
        rows = slice(row, row + LANES)
        high_ref[rows, :], low_ref[rows, :] = split(value_ref[rows, :])


def lateral(values, low, high, neighbours_ref, weight_ref):
    layers = len(values)
    rows, width = values[0].shape
    slots = neighbours_ref.shape[0]
    extended = [
        jnp.concatenate(
            [low[:, k * HW : (k + 1) * HW], values[k], high[:, k * HW : (k + 1) * HW]], axis=1
        )
        for k in range(layers)
    ]
    result = []
    for k in range(layers):
        blocks = []
        for block in range(width // LANES):
            lanes = slice(block * LANES, (block + 1) * LANES)
            first = extended[k][:, block * LANES : (block + 1) * LANES]
            second = extended[k][:, (block + 1) * LANES : (block + 2) * LANES]
            here = values[k][:, lanes]
            total = jnp.zeros((rows, LANES), F32)
            for slot in range(slots):
                index = neighbours_ref[slot : slot + 1, lanes] - block * LANES
                index = jnp.broadcast_to(index, (rows, LANES))
                inner = index & (LANES - 1)
                taken = jnp.where(
                    index < LANES,
                    jnp.take_along_axis(first, inner, axis=1, mode="promise_in_bounds"),
                    jnp.take_along_axis(second, inner, axis=1, mode="promise_in_bounds"),
                )
                total += weight_ref[slot, k : k + 1, lanes] * (here - taken)
            blocks.append(total)
        result.append(jnp.concatenate(blocks, axis=1))
    return result


def masked(flag, value):
    return jnp.where(flag, value, jnp.zeros_like(value))


def first_kernel(place, start_ref, rhs_ref, low_ref, high_ref, below_ref, neighbours_ref, weight_ref,
                 vert_ref, inv_high_ref, inv_low_ref, g_ref, total_ref):
    layers = start_ref.shape[0]
    depth, depths, area, areas = place()
    low = masked(area > 0, low_ref[...])
    high = masked(area < areas - 1, high_ref[...])
    below = masked(depth < depths - 1, below_ref[...])
    start = [start_ref[k] for k in range(layers)]
    lat = lateral(start, low, high, neighbours_ref, weight_ref)
    carried = None
    for k in range(layers):
        upper = vert_ref[k + 1 : k + 2, :] * start[k + 1] if k + 1 < layers else below
        g = rhs_ref[k] - lat[k] + upper
        g_ref[k] = g
        if carried is not None:
            g = g + vert_ref[k : k + 1, :] * carried
        carried = times(g, inv_high_ref[k], inv_low_ref[k])
    total_ref[...] = carried


def join_kernel(bit_of, up, own_ref, other_ref, own_high_ref, own_low_ref, other_high_ref,
                other_low_ref, total_ref):
    dims = NT if up else NN
    last = bit_of() == (0 if up else 1)

    @pl.when(last)
    def _():
        total_ref[...] = own_ref[...] + times(other_ref[...], own_high_ref[...], own_low_ref[...], dims)

    @pl.when(jnp.logical_not(last))
    def _():
        total_ref[...] = other_ref[...] + times(own_ref[...], other_high_ref[...], other_low_ref[...], dims)


def entering(bits, up, heard, products):
    value = None
    for level in reversed(range(len(heard))):
        later = bits[level] == (0 if up else 1)
        if value is None:
            value = masked(later, heard[level])
        else:
            high, low = products[level]
            value = jnp.where(
                later, heard[level] + times(value, high[...], low[...], NT if up else NN), value
            )
    return value


def down_kernel(bits_of, levels, g_ref, vert_ref, inv_high_ref, inv_low_ref, *refs):
    heard, refs = refs[:levels], refs[levels:]
    products, refs = refs[: 2 * (levels - 1)], refs[2 * (levels - 1) :]
    y_ref, entering_ref, left_ref, right_ref = refs
    layers, _, width = g_ref.shape
    pairs = [(products[2 * i], products[2 * i + 1]) for i in range(levels - 1)]
    carried = entering(bits_of(), False, [ref[...] for ref in heard], pairs)
    entering_ref[...] = carried
    for k in range(layers):
        carried = times(
            g_ref[k] + vert_ref[k : k + 1, :] * carried, inv_high_ref[k], inv_low_ref[k]
        )
        y_ref[k] = carried
    left_ref[...] = jnp.concatenate([y_ref[k, :, :HW] for k in range(layers)], axis=1)
    right_ref[...] = jnp.concatenate([y_ref[k, :, width - HW :] for k in range(layers)], axis=1)


def turn_kernel(place, y_ref, entering_ref, rhs_ref, low_ref, high_ref, neighbours_ref, weight_ref,
                vert_ref, inv_high_ref, inv_low_ref, h_ref, total_ref):
    layers = y_ref.shape[0]
    _, _, area, areas = place()
    low = masked(area > 0, low_ref[...])
    high = masked(area < areas - 1, high_ref[...])
    values = [y_ref[k] for k in range(layers)]
    lat = lateral(values, low, high, neighbours_ref, weight_ref)
    carried = None
    for k in reversed(range(layers)):
        vert = vert_ref[k : k + 1, :]
        h = rhs_ref[k] - lat[k] + vert * (values[k - 1] if k else entering_ref[...])
        h_ref[k] = h
        carried = vert * times(h if carried is None else h + carried, inv_high_ref[k], inv_low_ref[k], NT)
    total_ref[...] = carried


def up_kernel(bits_of, levels, h_ref, vert_ref, inv_high_ref, inv_low_ref, *refs):
    heard, refs = refs[:levels], refs[levels:]
    products, refs = refs[: 2 * (levels - 1)], refs[2 * (levels - 1) :]
    (updated_ref,) = refs
    layers = h_ref.shape[0]
    pairs = [(products[2 * i], products[2 * i + 1]) for i in range(levels - 1)]
    carried = entering(bits_of(), True, [ref[...] for ref in heard], pairs)
    for k in reversed(range(layers)):
        value = times(h_ref[k] + carried, inv_high_ref[k], inv_low_ref[k], NT)
        updated_ref[k] = value
        carried = vert_ref[k : k + 1, :] * value


def shards(rhs_field, start_field, inverses, facies, neighbours, lateral_table, vertical_table):
    layers, count, width = rhs_field.shape
    slots = neighbours.shape[1]
    depths, areas = lax.axis_size("depth"), lax.axis_size("area")
    levels = depths.bit_length() - 1
    assert depths == 1 << levels and levels >= 2

    def bit(level):
        return (lax.axis_index("depth") >> level) & 1

    def bits():
        return [bit(level) for level in range(levels)]

    def place():
        return lax.axis_index("depth"), depths, lax.axis_index("area"), areas

    def swapped(value, level):
        return lax.ppermute(value, "depth", [(i, i ^ (1 << level)) for i in range(depths)])

    def from_sides(left, right):
        low = lax.ppermute(right, "area", [(i, (i + 1) % areas) for i in range(areas)])
        high = lax.ppermute(left, "area", [((i + 1) % areas, i) for i in range(areas)])
        return low, high

    field = sds((layers, count, width))
    row = sds((count, width))
    matrix, matrix16 = sds((width, width)), sds((width, width), BF16)
    edge = sds((count, layers * HW))
    flops = 2 * width * width
    neighbour_rows = neighbours.T

    left, right, top = call(
        edges_kernel, "edges", (edge, edge, row), [VMEM, VMEM, SMEM], 4, 1 << 16, 1 << 18
    )(start_field, facies, vertical_table)
    low, high = from_sides(left, right)
    below = lax.ppermute(top, "depth", [((i + 1) % depths, i) for i in range(depths)])

    inv16 = sds((layers, width, width), BF16)
    inv_high, inv_low, product, product_high, product_low, weight, vert = call(
        setup_kernel, "setup",
        (inv16, inv16, matrix, matrix16, matrix16, sds((slots, layers, width)), sds((layers, width))),
        [VMEM, VMEM, SMEM, SMEM], 16, 3 * (layers - 1) * flops * width, 8 << 20,
    )(inverses, facies, lateral_table, vertical_table)

    own = [(product_high, product_low)]
    other = []
    for level in range(levels - 1):
        arrived = swapped(product, level)
        if level < levels - 2:
            other_high, other_low, product, product_high, product_low = call(
                functools.partial(pair_kernel, functools.partial(bit, level)), f"pair{level}",
                (matrix16, matrix16, matrix, matrix16, matrix16), [VMEM] * 4, 16,
                3 * flops * width, 6 << 20,
            )(product, product_high, product_low, arrived)
            own.append((product_high, product_low))
        else:
            other_high, other_low = call(
                split_kernel, f"split{level}", (matrix16, matrix16), [VMEM], 8, 1 << 20, 2 << 20
            )(arrived)
        other.append((other_high, other_low))

    g, total = call(
        functools.partial(first_kernel, place), "first", (field, row), [VMEM] * 10, 8,
        3 * layers * count * flops, 4 << 20,
    )(start_field, rhs_field, low, high, below, neighbour_rows, weight, vert, inv_high, inv_low)

    def exchange(total, up):
        heard = []
        for level in range(levels):
            heard.append(swapped(total, level))
            if level < levels - 1:
                total = call(
                    functools.partial(join_kernel, functools.partial(bit, level), up),
                    f"join{'up' if up else 'down'}{level}", row, [VMEM] * 6, 8,
                    3 * count * flops, 2 << 20,
                )(total, heard[level], *own[level], *other[level])
        return heard

    partners = [part for pair in other for part in pair]
    heard = exchange(total, False)
    y, came, left, right = call(
        functools.partial(down_kernel, bits, levels), "down", (field, row, edge, edge),
        [VMEM] * (4 + levels + 2 * (levels - 1)), 16, 9 * layers * count * flops, 6 << 20,
    )(g, vert, inv_high, inv_low, *heard, *partners)
    low, high = from_sides(left, right)
    h, total = call(
        functools.partial(turn_kernel, place), "turn", (field, row), [VMEM] * 10, 8,
        3 * layers * count * flops, 4 << 20,
    )(y, came, rhs_field, low, high, neighbour_rows, weight, vert, inv_high, inv_low)
    heard = exchange(total, True)
    return call(
        functools.partial(up_kernel, bits, levels), "up", field,
        [VMEM] * (4 + levels + 2 * (levels - 1)), 16, 9 * layers * count * flops, 6 << 20,
    )(h, vert, inv_high, inv_low, *heard, *partners)


def solution(mesh):
    return jax.shard_map(
        shards,
        mesh=mesh,
        in_specs=(
            P("depth", None, "area"),
            P("depth", None, "area"),
            P("depth", "area", None),
            P("depth", "area"),
            P("area", None),
            P(),
            P(),
        ),
        out_specs=P("depth", None, "area"),
        check_vma=False,
    )
```

time: 186 us -> 69.3 us (0.37)
  the two profiles are of different devices: /device:TPU:19 before, /device:TPU:0 now
where the time goes in v1:
time: 69.3 us; the launch traced here: 69.1 us
  waiting for transfers between devices  36 us (52%)
  starting transfers between devices  18.9 us (27%)
  Pallas kernels  10.4 us (15%)
  local copies, waits for them, and re-layouts  3.72 us (5%)
    ppermute x8, waiting for transfers between devices, swapped(): lax.ppermute(value, 'depth', [(i, i ^ 1 << level) for i in range(depths)])  16.3 us
    ppermute x1, waiting for transfers between devices, shards(): lax.ppermute(top, 'depth', [((i + 1) % depths, i) for i in range(depths)])  16.2 us
    ppermute x8, starting transfers between devices, swapped(): lax.ppermute(value, 'depth', [(i, i ^ 1 << level) for i in range(depths)])  10.3 us
    ppermute x2, starting transfers between devices, from_sides(): lax.ppermute(left, 'area', [((i + 1) % areas, i) for i in range(areas)])  4.49 us
    unnamed x17, local copies, waits for them, and re-layouts  3.72 us
    ppermute x2, waiting for transfers between devices, from_sides(): lax.ppermute(right, 'area', [(i, (i + 1) % areas) for i in range(areas)])  3.5 us
    ppermute x2, starting transfers between devices, from_sides(): lax.ppermute(right, 'area', [(i, (i + 1) % areas) for i in range(areas)])  3.18 us
    pallas_call x1, Pallas kernels, shards(): call(functools.partial(up_kernel, bits, levels), 'up', field, [VMEM] * (4...  2.14 us
  transfers between devices with their start and end apart: 13, of which 10 were waited for; matrix products, arithmetic and copies ran while one was open for 0% of the time, Pallas kernels for 3%

profile of v1, /device:TPU:0, one launch (start us, length us, event | category | flops | bytes accessed | tf_op | source)
XLA Modules:
  0.0 69.1 jit_solution(11328691565692117053)
XLA Ops:
  2.1 1.6 %copy-done.7 = f32[2,512,512]{2,1,0:T(8,128)S(1)} copy-done((f32[2,512,512]{2,1,0:T(8,128)S(1)}, f32[2,512,512]{2,1,0:T(8,128)}, u32[]{:S(2)}) %copy-start.7) | copy-done | bytes 2097176
  3.7 1.9 %setup.1 = (bf16[2,512,512]{2,1,0:T(8,128)(2,1)S(1)}, bf16[2,512,512]{2,1,0:T(8,128)(2,1)S(1)}, f32[512,512]{1,0:T(8,128)S(1)}, bf16[512,512]{1,0:T(8,128)(2,1)S...) custom-call(f32[2,512,512]{2,1,0:T(8,128)S(1)} %copy-done.7, ...), custom_call_target="tpu_custom_call" | custom-call | flops 805306368 | bytes 8388608 | tf_op jit(solution)/shard_map/setup/pallas_call | solution.py:295
  6.2 2.3 %collective-permute-done.4.other_ref = f32[512,512]{1,0:T(8,128)S(1)} collective-permute-done((f32[512,512]{1,0:T(8,128)S(1)}, f32[512,512]{1,0:T(8,128)S(1)}, u32[]{:S(2)}, u32[]{:S(2)}) %collective-permute-start.4) | collective-permute-done | bytes 1048608 | tf_op jit(solution)/shard_map/ppermute | solution.py:274
  8.5 1.2 %pair0.1 = (bf16[512,512]{1,0:T(8,128)(2,1)S(1)}, bf16[512,512]{1,0:T(8,128)(2,1)S(1)}, f32[512,512]{1,0:T(8,128)S(1)}, bf16[512,512]{1,0:T(8,128)(2,1)S(1)}, bf16[512,512]{1,0:T(8,128)(2,1)S(1)}) custom-call(f32[512,512]{1,0:T(8,128)S(1)} %get-tuple-element.41.own_ref, bf16[512,512]{1,0:T(8,128)(2,1)S(1)} %get-tuple-element.39.own_high_ref, ...), custom_call_target="tpu_custom_call" | custom-call | flops 805306368 | bytes 6291456 | tf_op jit(solution)/shard_map/pair0/pallas_call | solution.py:306
  9.7 2.9 %collective-permute-start.6 = (f32[512,512]{1,0:T(8,128)S(1)}, f32[512,512]{1,0:T(8,128)S(1)}, u32[]{:S(2)}, u32[]{:S(2)}) collective-permute-start(f32[512,512]{1,0:T(8,128)S(1)} %get-tuple-element.46), channel_id=1, source_target_pairs={{0,8},{4,12},{8,0},{12,4},{16,24},{20,28},{24,16},{28,20},{1,9},{5... | collective-permute-start | bytes 3145736 | tf_op jit(solution)/shard_map/ppermute | solution.py:274
  13.2 1.0 %collective-permute-start.2 = (f32[32,512]{1,0:T(8,128)S(1)}, f32[32,512]{1,0:T(8,128)S(1)}, u32[]{:S(2)}, u32[]{:S(2)}) collective-permute-start(f32[32,512]{1,0:T(8,128)S(1)} %get-tuple-element.32), channel_id=1, source_target_pairs={{4,0},{8,4},{12,8},{16,12},{20,16},{24,20},{28,24},{0,28},{5,1},{9... | collective-permute-start | bytes 196616 | tf_op jit(solution)/shard_map/ppermute | solution.py:292
  14.2 1.6 %collective-permute-start = (f32[32,128]{1,0:T(8,128)S(1)}, f32[32,128]{1,0:T(8,128)S(1)}, u32[]{:S(2)}, u32[]{:S(2)}) collective-permute-start(f32[32,128]{1,0:T(8,128)S(1)} %get-tuple-element.30), channel_id=1, source_target_pairs={{0,1},{1,2},{2,3},{3,0},{4,5},{5,6},{6,7},{7,4},{8,9},{9,10},{10,1... | collective-permute-start | bytes 49160 | tf_op jit(solution)/shard_map/ppermute | solution.py:277
  15.8 2.2 %collective-permute-start.1 = (f32[32,128]{1,0:T(8,128)S(1)}, f32[32,128]{1,0:T(8,128)S(1)}, u32[]{:S(2)}, u32[]{:S(2)}) collective-permute-start(f32[32,128]{1,0:T(8,128)S(1)} %get-tuple-element.31), channel_id=1, source_target_pairs={{1,0},{2,1},{3,2},{0,3},{5,4},{6,5},{7,6},{4,7},{9,8},{10,9},{11,1... | collective-permute-start | bytes 49160 | tf_op jit(solution)/shard_map/ppermute | solution.py:278
  18.0 1.8 %collective-permute-done.low_ref = f32[32,128]{1,0:T(8,128)S(1)} collective-permute-done((f32[32,128]{1,0:T(8,128)S(1)}, f32[32,128]{1,0:T(8,128)S(1)}, u32[]{:S(2)}, u32[]{:S(2)}) %collective-permute-start) | collective-permute-done | bytes 16416 | tf_op jit(solution)/shard_map/ppermute | solution.py:277
  19.8 16.2 %collective-permute-done.2.below_ref = f32[32,512]{1,0:T(8,128)S(1)} collective-permute-done((f32[32,512]{1,0:T(8,128)S(1)}, f32[32,512]{1,0:T(8,128)S(1)}, u32[]{:S(2)}, u32[]{:S(2)}) %collective-permute-start.2) | collective-permute-done | bytes 65568 | tf_op jit(solution)/shard_map/ppermute | solution.py:292
  37.4 0.9 %collective-permute-done.3.other_ref.refs_0_ = f32[32,512]{1,0:T(8,128)S(1)} collective-permute-done((f32[32,512]{1,0:T(8,128)S(1)}, f32[32,512]{1,0:T(8,128)S(1)}, u32[]{:S(2)}, u32[]{:S(2)}) %collective-permute-start.3) | collective-permute-done | bytes 65568 | tf_op jit(solution)/shard_map/ppermute | solution.py:274
  38.6 2.7 %collective-permute-start.5 = (f32[32,512]{1,0:T(8,128)S(1)}, f32[32,512]{1,0:T(8,128)S(1)}, u32[]{:S(2)}, u32[]{:S(2)}) collective-permute-start(f32[32,512]{1,0:T(8,128)S(1)} %joindown0.1.own_ref), channel_id=1, source_target_pairs={{0,8},{4,12},{8,0},{12,4},{16,24},{20,28},{24,16},{28,20},{1,9},{5... | collective-permute-start | bytes 196616 | tf_op jit(solution)/shard_map/ppermute | solution.py:274
  41.5 2.4 %collective-permute-done.5.other_ref.refs_1_ = f32[32,512]{1,0:T(8,128)S(1)} collective-permute-done((f32[32,512]{1,0:T(8,128)S(1)}, f32[32,512]{1,0:T(8,128)S(1)}, u32[]{:S(2)}, u32[]{:S(2)}) %collective-permute-start.5) | collective-permute-done | bytes 65568 | tf_op jit(solution)/shard_map/ppermute | solution.py:274
  45.0 3.4 %collective-permute-done.7.refs_2_ = f32[32,512]{1,0:T(8,128)S(1)} collective-permute-done((f32[32,512]{1,0:T(8,128)S(1)}, f32[32,512]{1,0:T(8,128)S(1)}, u32[]{:S(2)}, u32[]{:S(2)}) %collective-permute-start.7) | collective-permute-done | bytes 65568 | tf_op jit(solution)/shard_map/ppermute | solution.py:274
  48.5 1.1 %down.1 = (f32[2,32,512]{2,1,0:T(8,128)S(1)}, f32[32,512]{1,0:T(8,128)S(1)}, f32[32,128]{1,0:T(8,128)S(1)}, f32[32,128]{1,0:T(8,128)S(1)}) custom-call(f32[2,32,512]{2,1,0:T(8,128)S(1)} %get-tuple-element.37.g_ref, f32[2,512]{1,0:T(2,128)S(1)} %get-tuple-element.34.vert_ref, bf16[2,512,512]{2,1,0:T(8,128)(2,1)S(1)} %get-tuple-element.35.inv_high_ref, ...), custom_call_target="tpu_custom_call" | custom-call | flops 301989888 | bytes 6291456 | tf_op jit(solution)/shard_map/down/pallas_call | solution.py:337
  49.6 1.6 %collective-permute-start.8 = (f32[32,128]{1,0:T(8,128)S(1)}, f32[32,128]{1,0:T(8,128)S(1)}, u32[]{:S(2)}, u32[]{:S(2)}) collective-permute-start(f32[32,128]{1,0:T(8,128)S(1)} %get-tuple-element.51), channel_id=1, source_target_pairs={{0,1},{1,2},{2,3},{3,0},{4,5},{5,6},{6,7},{7,4},{8,9},{9,10},{10,1... | collective-permute-start | bytes 49160 | tf_op jit(solution)/shard_map/ppermute | solution.py:277
  51.2 2.2 %collective-permute-start.9 = (f32[32,128]{1,0:T(8,128)S(1)}, f32[32,128]{1,0:T(8,128)S(1)}, u32[]{:S(2)}, u32[]{:S(2)}) collective-permute-start(f32[32,128]{1,0:T(8,128)S(1)} %get-tuple-element.52), channel_id=1, source_target_pairs={{1,0},{2,1},{3,2},{0,3},{5,4},{6,5},{7,6},{4,7},{9,8},{10,9},{11,1... | collective-permute-start | bytes 49160 | tf_op jit(solution)/shard_map/ppermute | solution.py:278
  53.4 1.7 %collective-permute-done.8.low_ref = f32[32,128]{1,0:T(8,128)S(1)} collective-permute-done((f32[32,128]{1,0:T(8,128)S(1)}, f32[32,128]{1,0:T(8,128)S(1)}, u32[]{:S(2)}, u32[]{:S(2)}) %collective-permute-start.8) | collective-permute-done | bytes 16416 | tf_op jit(solution)/shard_map/ppermute | solution.py:277
  55.2 1.1 %turn.1 = (f32[2,32,512]{2,1,0:T(8,128)S(1)}, f32[32,512]{1,0:T(8,128)S(1)}) custom-call(f32[2,32,512]{2,1,0:T(8,128)S(1)} %get-tuple-element.49.y_ref, f32[32,512]{1,0:T(8,128)S(1)} %get-tuple-element.50.entering_ref, f32[2,32,512]{2,1,0:T(8,128)S(1)} %copy-done, f32[32,128]{1,0:T(8,128)S(1)} %collective-permute-done.8.low_ref, ...), custom_call_target="tpu_custom_call" | custom-call | flops 100663296 | bytes 4194304 | tf_op jit(solution)/shard_map/turn/pallas_call | solution.py:342
  56.3 1.2 %collective-permute-done.10.other_ref.refs_0_ = f32[32,512]{1,0:T(8,128)S(1)} collective-permute-done((f32[32,512]{1,0:T(8,128)S(1)}, f32[32,512]{1,0:T(8,128)S(1)}, u32[]{:S(2)}, u32[]{:S(2)}) %collective-permute-start.10) | collective-permute-done | bytes 65568 | tf_op jit(solution)/shard_map/ppermute | solution.py:274
  58.0 1.8 %collective-permute-start.11 = (f32[32,512]{1,0:T(8,128)S(1)}, f32[32,512]{1,0:T(8,128)S(1)}, u32[]{:S(2)}, u32[]{:S(2)}) collective-permute-start(f32[32,512]{1,0:T(8,128)S(1)} %joinup0.1.own_ref), channel_id=1, source_target_pairs={{0,8},{4,12},{8,0},{12,4},{16,24},{20,28},{24,16},{28,20},{1,9},{5... | collective-permute-start | bytes 196616 | tf_op jit(solution)/shard_map/ppermute | solution.py:274
  59.7 2.5 %collective-permute-done.11.other_ref.refs_1_ = f32[32,512]{1,0:T(8,128)S(1)} collective-permute-done((f32[32,512]{1,0:T(8,128)S(1)}, f32[32,512]{1,0:T(8,128)S(1)}, u32[]{:S(2)}, u32[]{:S(2)}) %collective-permute-start.11) | collective-permute-done | bytes 65568 | tf_op jit(solution)/shard_map/ppermute | solution.py:274
  63.5 3.4 %collective-permute-done.12.refs_2_ = f32[32,512]{1,0:T(8,128)S(1)} collective-permute-done((f32[32,512]{1,0:T(8,128)S(1)}, f32[32,512]{1,0:T(8,128)S(1)}, u32[]{:S(2)}, u32[]{:S(2)}) %collective-permute-start.12) | collective-permute-done | bytes 65568 | tf_op jit(solution)/shard_map/ppermute | solution.py:274
  67.0 2.1 %up.1 = f32[2,32,512]{2,1,0:T(8,128)} custom-call(f32[2,32,512]{2,1,0:T(8,128)S(1)} %get-tuple-element.53.h_ref, f32[2,512]{1,0:T(2,128)S(1)} %get-tuple-element.34.vert_ref, bf16[2,512,512]{2,1,0:T(8,128)(2,1)S(1)} %get-tuple-element.35.inv_high_ref, bf16[2,512,512]{2,1,0:T(8,128)(2,1)S(1)} %get-tuple-element.36.inv_low_ref, ...), custom_call_target="tpu_custom_call" | custom-call | flops 301989888 | bytes 6291456 | tf_op jit(solution)/shard_map/up/pallas_call | solution.py:347
  (31 shorter events, 8.0 us)
Async XLA Ops:
  0.8 0.7 copy-start.3
  1.4 0.7 copy-start.5
  2.1 1.6 %copy-start.7 = (f32[2,512,512]{2,1,0:T(8,128)S(1)}, f32[2,512,512]{2,1,0:T(8,128)}, u32[]{:S(2)}) copy-start(f32[2,512,512]{2,1,0:T(8,128)} %inverses_ref.1) | copy-start | bytes 6291460
  5.6 7.0 %copy-start.1 = (f32[2,32,512]{2,1,0:T(8,128)S(1)}, f32[2,32,512]{2,1,0:T(8,128)}, u32[]{:S(2)}) copy-start(f32[2,32,512]{2,1,0:T(8,128)} %start_ref.3) | copy-start | bytes 393220
  5.6 7.0 %copy-start.4 = (s32[2,512]{1,0:T(2,128)S(1)}, s32[2,512]{1,0:T(2,128)}, u32[]{:S(2)}) copy-start(s32[2,512]{1,0:T(2,128)} %facies_ref.3) | copy-start | bytes 12292
  5.6 7.0 %copy-start.6 = (f32[8]{0:T(128)S(1)}, f32[8]{0:T(128)}, u32[]{:S(2)}) copy-start(f32[8]{0:T(128)} %vertical_ref.3) | copy-start | bytes 100
  5.6 30.4 %copy-start = (f32[2,32,512]{2,1,0:T(8,128)S(1)}, f32[2,32,512]{2,1,0:T(8,128)}, u32[]{:S(2)}) copy-start(f32[2,32,512]{2,1,0:T(8,128)} %rhs_ref.3) | copy-start | bytes 393220
  5.6 30.4 %copy-start.2 = (s32[512,4]{0,1:T(4,128)S(1)}, s32[512,4]{0,1:T(4,128)}, u32[]{:S(2)}) copy-start(s32[512,4]{0,1:T(4,128)} %param.11) | copy-start | bytes 24580
  5.7 2.8 %collective-permute-start.4 = (f32[512,512]{1,0:T(8,128)S(1)}, f32[512,512]{1,0:T(8,128)S(1)}, u32[]{:S(2)}, u32[]{:S(2)}) collective-permute-start(f32[512,512]{1,0:T(8,128)S(1)} %get-tuple-element.41.own_ref), channel_id=1, source_target_pairs={{0,4},{4,0},{8,12},{12,8},{16,20},{20,16},{24,28},{28,24},{1,5},{5... | collective-permute-start | bytes 3145736 | tf_op jit(solution)/shard_map/ppermute | solution.py:274
  9.7 31.7 %collective-permute-start.6 = (f32[512,512]{1,0:T(8,128)S(1)}, f32[512,512]{1,0:T(8,128)S(1)}, u32[]{:S(2)}, u32[]{:S(2)}) collective-permute-start(f32[512,512]{1,0:T(8,128)S(1)} %get-tuple-element.46), channel_id=1, source_target_pairs={{0,8},{4,12},{8,0},{12,4},{16,24},{20,28},{24,16},{28,20},{1,9},{5... | collective-permute-start | bytes 3145736 | tf_op jit(solution)/shard_map/ppermute | solution.py:274
  13.2 22.8 %collective-permute-start.2 = (f32[32,512]{1,0:T(8,128)S(1)}, f32[32,512]{1,0:T(8,128)S(1)}, u32[]{:S(2)}, u32[]{:S(2)}) collective-permute-start(f32[32,512]{1,0:T(8,128)S(1)} %get-tuple-element.32), channel_id=1, source_target_pairs={{4,0},{8,4},{12,8},{16,12},{20,16},{24,20},{28,24},{0,28},{5,1},{9... | collective-permute-start | bytes 196616 | tf_op jit(solution)/shard_map/ppermute | solution.py:292
  14.2 5.6 %collective-permute-start = (f32[32,128]{1,0:T(8,128)S(1)}, f32[32,128]{1,0:T(8,128)S(1)}, u32[]{:S(2)}, u32[]{:S(2)}) collective-permute-start(f32[32,128]{1,0:T(8,128)S(1)} %get-tuple-element.30), channel_id=1, source_target_pairs={{0,1},{1,2},{2,3},{3,0},{4,5},{5,6},{6,7},{7,4},{8,9},{9,10},{10,1... | collective-permute-start | bytes 49160 | tf_op jit(solution)/shard_map/ppermute | solution.py:277
  15.8 4.0 %collective-permute-start.1 = (f32[32,128]{1,0:T(8,128)S(1)}, f32[32,128]{1,0:T(8,128)S(1)}, u32[]{:S(2)}, u32[]{:S(2)}) collective-permute-start(f32[32,128]{1,0:T(8,128)S(1)} %get-tuple-element.31), channel_id=1, source_target_pairs={{1,0},{2,1},{3,2},{0,3},{5,4},{6,5},{7,6},{4,7},{9,8},{10,9},{11,1... | collective-permute-start | bytes 49160 | tf_op jit(solution)/shard_map/ppermute | solution.py:278
  36.8 1.5 %collective-permute-start.3 = (f32[32,512]{1,0:T(8,128)S(1)}, f32[32,512]{1,0:T(8,128)S(1)}, u32[]{:S(2)}, u32[]{:S(2)}) collective-permute-start(f32[32,512]{1,0:T(8,128)S(1)} %get-tuple-element.38.own_ref), channel_id=1, source_target_pairs={{0,4},{4,0},{8,12},{12,8},{16,20},{20,16},{24,28},{28,24},{1,5},{5... | collective-permute-start | bytes 196616 | tf_op jit(solution)/shard_map/ppermute | solution.py:274
  38.6 5.3 %collective-permute-start.5 = (f32[32,512]{1,0:T(8,128)S(1)}, f32[32,512]{1,0:T(8,128)S(1)}, u32[]{:S(2)}, u32[]{:S(2)}) collective-permute-start(f32[32,512]{1,0:T(8,128)S(1)} %joindown0.1.own_ref), channel_id=1, source_target_pairs={{0,8},{4,12},{8,0},{12,4},{16,24},{20,28},{24,16},{28,20},{1,9},{5... | collective-permute-start | bytes 196616 | tf_op jit(solution)/shard_map/ppermute | solution.py:274
  44.2 4.3 %collective-permute-start.7 = (f32[32,512]{1,0:T(8,128)S(1)}, f32[32,512]{1,0:T(8,128)S(1)}, u32[]{:S(2)}, u32[]{:S(2)}) collective-permute-start(f32[32,512]{1,0:T(8,128)S(1)} %joindown1.1), channel_id=1, source_target_pairs={{0,16},{4,20},{8,24},{12,28},{16,0},{20,4},{24,8},{28,12},{1,17},{... | collective-permute-start | bytes 196616 | tf_op jit(solution)/shard_map/ppermute | solution.py:274
  49.6 5.6 %collective-permute-start.8 = (f32[32,128]{1,0:T(8,128)S(1)}, f32[32,128]{1,0:T(8,128)S(1)}, u32[]{:S(2)}, u32[]{:S(2)}) collective-permute-start(f32[32,128]{1,0:T(8,128)S(1)} %get-tuple-element.51), channel_id=1, source_target_pairs={{0,1},{1,2},{2,3},{3,0},{4,5},{5,6},{6,7},{7,4},{8,9},{9,10},{10,1... | collective-permute-start | bytes 49160 | tf_op jit(solution)/shard_map/ppermute | solution.py:277
  51.2 4.0 %collective-permute-start.9 = (f32[32,128]{1,0:T(8,128)S(1)}, f32[32,128]{1,0:T(8,128)S(1)}, u32[]{:S(2)}, u32[]{:S(2)}) collective-permute-start(f32[32,128]{1,0:T(8,128)S(1)} %get-tuple-element.52), channel_id=1, source_target_pairs={{1,0},{2,1},{3,2},{0,3},{5,4},{6,5},{7,6},{4,7},{9,8},{10,9},{11,1... | collective-permute-start | bytes 49160 | tf_op jit(solution)/shard_map/ppermute | solution.py:278
  56.3 1.3 %collective-permute-start.10 = (f32[32,512]{1,0:T(8,128)S(1)}, f32[32,512]{1,0:T(8,128)S(1)}, u32[]{:S(2)}, u32[]{:S(2)}) collective-permute-start(f32[32,512]{1,0:T(8,128)S(1)} %get-tuple-element.54.own_ref), channel_id=1, source_target_pairs={{0,4},{4,0},{8,12},{12,8},{16,20},{20,16},{24,28},{28,24},{1,5},{5... | collective-permute-start | bytes 196616 | tf_op jit(solution)/shard_map/ppermute | solution.py:274
  58.0 4.3 %collective-permute-start.11 = (f32[32,512]{1,0:T(8,128)S(1)}, f32[32,512]{1,0:T(8,128)S(1)}, u32[]{:S(2)}, u32[]{:S(2)}) collective-permute-start(f32[32,512]{1,0:T(8,128)S(1)} %joinup0.1.own_ref), channel_id=1, source_target_pairs={{0,8},{4,12},{8,0},{12,4},{16,24},{20,28},{24,16},{28,20},{1,9},{5... | collective-permute-start | bytes 196616 | tf_op jit(solution)/shard_map/ppermute | solution.py:274
  62.7 4.3 %collective-permute-start.12 = (f32[32,512]{1,0:T(8,128)S(1)}, f32[32,512]{1,0:T(8,128)S(1)}, u32[]{:S(2)}, u32[]{:S(2)}) collective-permute-start(f32[32,512]{1,0:T(8,128)S(1)} %joinup1.1), channel_id=1, source_target_pairs={{0,16},{4,20},{8,24},{12,28},{16,0},{20,4},{24,8},{28,12},{1,17},{... | collective-permute-start | bytes 196616 | tf_op jit(solution)/shard_map/ppermute | solution.py:274
